TPU v7x, 32 devices: a whole 2x2x4 slice. The times are simulated.
32 devices in a mesh: fsdp: 8 (over y, x, core), tp: 4 (over z).
Axes of the slice: x: 2, y: 2, z: 4, core: 2. Of those that a mesh axis runs over, the one named last changes fastest.
Arguments:
- tokens: bfloat16 [2, 2048, 2048], P(None, 'fsdp', 'tp'), may hold values from -6 to 6
- out_grad: bfloat16 [2, 2048, 2048], P(None, 'fsdp', 'tp'), may hold values from -6 to 6
- segment_ids: int32 [2, 2048], P(None, 'fsdp'), may hold values from 0 to 3, as said below
- positions: int32 [2, 2048], P(None, 'fsdp'), may hold values from 0 to 1023, as said below
- attn_norm: bfloat16 [2048], P('fsdp'), may hold values from 0.25 to 1.75
- w_query: bfloat16 [2048, 2048], P('fsdp', 'tp'), may hold values from -0.125 to 0.125
- key_projection_weight: bfloat16 [2048, 256], P('fsdp', 'tp'), may hold values from -0.125 to 0.125
- value_projection_weight: bfloat16 [2048, 256], P('fsdp', 'tp'), may hold values from -0.125 to 0.125
- w_out: bfloat16 [2048, 2048], P('tp', 'fsdp'), may hold values from -1 to 1
- mlp_norm: bfloat16 [2048], P('fsdp'), may hold values from 0.25 to 1.75
- w_gate: bfloat16 [2048, 5632], P('fsdp', 'tp'), may hold values from -0.125 to 0.125
- w_up: bfloat16 [2048, 5632], P('fsdp', 'tp'), may hold values from -0.125 to 0.125
- w_down: bfloat16 [5632, 2048], P('tp', 'fsdp'), may hold values from -0.078125 to 0.078125
Outputs:
- layer_out: bfloat16 [2, 2048, 2048], P(None, 'fsdp', 'tp')
- input_grad: float32 [2, 2048, 2048], P(None, 'fsdp', 'tp')
- grad_attn_norm: float32 [2048], P('fsdp')
- grad_query: float32 [2048, 2048], P('fsdp', 'tp')
- grad_key: float32 [2048, 256], P('fsdp', 'tp')
- grad_value: float32 [2048, 256], P('fsdp', 'tp')
- grad_out: float32 [2048, 2048], P('tp', 'fsdp')
- grad_mlp_norm: float32 [2048], P('fsdp')
- grad_gate: float32 [2048, 5632], P('fsdp', 'tp')
- grad_up: float32 [2048, 5632], P('fsdp', 'tp')
- grad_down: float32 [5632, 2048], P('tp', 'fsdp')
Inputs may be any that keep to these rules, and one draw needn't show every extreme that they name: `segment_ids`: within each sequence of 2048 tokens, taken in its own order, the ids run 0, 1, 2, 3 in order, each a contiguous run of 1 token or more; one run in each sequence is exactly 1024 tokens long. `positions`: each token's offset, in its sequence's order, from the first token of its run of equal segment_ids.
All inputs are finite; a program needn't handle non-finite values.
Results may differ from a plain program's by a relative error of at most 0.014.
Values may be sent and summed in bfloat16 or wider, within the bound.
No kernel may reach another device: no remote copies, remote signals or barrier semaphores. Data moves between devices by JAX's collectives and lax.ppermute only.
A program may use at most 256 MiB of HBM per device.

v0:
```python
import jax
import jax.numpy as jnp
from jax import lax
from jax.sharding import PartitionSpec as P

HEAD_SIZE = 64
SEQUENCE_LENGTH = 2048


NORM_EPSILON = 1e-05
ROPE_BASE = 10000.0
MASKED_SCORE = -1e30


def passed_along(block, axis, distance):
    devices = range(lax.axis_size(axis))
    route = [(i - distance, i) for i in devices if i - distance in devices]
    return lax.ppermute(block, axis, route)


def rope_tables(offsets, head_width):
    half_width = head_width // 2
    inverse = ROPE_BASE ** (-(jnp.arange(half_width, dtype=jnp.float32) * 2.0 / head_width))
    angles = offsets.astype(jnp.float32)[:, None] * inverse[None, :]
    cosine_table = jnp.concatenate([jnp.cos(angles), jnp.cos(angles)], -1)
    sine_lookup = jnp.concatenate([jnp.sin(angles), jnp.sin(angles)], -1)
    return (cosine_table, sine_lookup)


def apply_rotary(vectors, cosine_table, sine_lookup):
    half_width = vectors.shape[-1] // 2
    turned = jnp.concatenate([-vectors[..., half_width:], vectors[..., :half_width]], -1)
    return vectors * cosine_table[:, None, :] + turned * sine_lookup[:, None, :]


def reverse_rotary(cotangent, cosine_table, sine_lookup):
    half_width = cotangent.shape[-1] // 2
    scaled = cotangent * sine_lookup[:, None, :]
    return cotangent * cosine_table[:, None, :] + jnp.concatenate(
        [scaled[..., half_width:], -scaled[..., :half_width]], -1
    )


def outer_sum(left_rows, right_rows):
    return lax.dot_general(
        left_rows, right_rows, (((0,), (0,)), ((), ())), preferred_element_type=jnp.float32
    )


def transposed_product(left_rows, right_rows):
    return lax.dot_general(
        left_rows, right_rows, (((1,), (1,)), ((), ())), preferred_element_type=jnp.float32
    )


def full_width(local_part):
    return lax.all_gather(local_part, "tp", axis=1, tiled=True)


def width_sum(partial_term):
    return lax.psum_scatter(partial_term, "tp", scatter_dimension=1, tiled=True)


def back_sum(partial_term):
    return lax.psum(partial_term, "tp")


def block_scores(query_rotated, key_rows, score_scale):
    return (
        jnp.einsum("lhd,md->hlm", query_rotated, key_rows, preferred_element_type=jnp.float32)
        * score_scale
    )


def block_mask(query_segments, query_index, key_segments, key_index, usable):
    same_doc = query_segments[:, None] == key_segments[None, :]
    causal = key_index[None, :] <= query_index[:, None]
    return (same_doc & causal & usable)[None]


def attend_forward(query_rotated, key_blocks, query_segments, query_index, score_scale):
    row_count, head_count, head_width = query_rotated.shape
    running_max = jnp.full((head_count, row_count), MASKED_SCORE, jnp.float32)
    running_sum = jnp.zeros((head_count, row_count), jnp.float32)
    for key_rows, value_rows, key_segments, key_index, usable in key_blocks:
        scores = block_scores(query_rotated, key_rows, score_scale)
        allowed = block_mask(query_segments, query_index, key_segments, key_index, usable)
        block_max = jnp.max(jnp.where(allowed, scores, MASKED_SCORE), -1)
        new_max = jnp.maximum(running_max, block_max)
        running_sum = running_sum * jnp.exp(running_max - new_max) + jnp.sum(
            jnp.where(allowed, jnp.exp(scores - new_max[..., None]), 0.0), -1
        )
        running_max = new_max
    log_total = running_max + jnp.log(running_sum)
    heads_sum = jnp.zeros((row_count, head_count, head_width), jnp.float32)
    for key_rows, value_rows, key_segments, key_index, usable in key_blocks:
        scores = block_scores(query_rotated, key_rows, score_scale)
        allowed = block_mask(query_segments, query_index, key_segments, key_index, usable)
        prob_round = jnp.where(allowed, jnp.exp(scores - log_total[..., None]), 0.0).astype(
            jnp.bfloat16
        )
        heads_sum = heads_sum + jnp.einsum(
            "hlm,md->lhd", prob_round, value_rows, preferred_element_type=jnp.float32
        )
    return (heads_sum.astype(jnp.bfloat16), log_total)


def attend_backward(
    query_rotated,
    key_blocks,
    query_segments,
    query_index,
    log_total,
    heads_low,
    grad_low,
    score_scale,
):
    delta = jnp.sum(grad_low.astype(jnp.float32) * heads_low.astype(jnp.float32), -1).T
    grad_query = jnp.zeros(query_rotated.shape, jnp.float32)
    block_grads = []
    for key_rows, value_rows, key_segments, key_index, usable in key_blocks:
        scores = block_scores(query_rotated, key_rows, score_scale)
        allowed = block_mask(query_segments, query_index, key_segments, key_index, usable)
        prob_exact = jnp.where(allowed, jnp.exp(scores - log_total[..., None]), 0.0)
        prob_round = prob_exact.astype(jnp.bfloat16)
        grad_values = jnp.einsum(
            "hlm,lhd->md", prob_round, grad_low, preferred_element_type=jnp.float32
        )
        grad_probs = jnp.einsum(
            "lhd,md->hlm", grad_low, value_rows, preferred_element_type=jnp.float32
        )
        grad_scores = (prob_exact * (grad_probs - delta[..., None]) * score_scale).astype(
            jnp.bfloat16
        )
        grad_query = grad_query + jnp.einsum(
            "hlm,md->lhd", grad_scores, key_rows, preferred_element_type=jnp.float32
        )
        grad_keys = jnp.einsum(
            "hlm,lhd->md", grad_scores, query_rotated, preferred_element_type=jnp.float32
        )
        block_grads.append((grad_keys, grad_values))
    return (grad_query, block_grads)


def shards(
    tokens,
    out_grad,
    segment_ids,
    positions,
    attn_norm,
    w_query,
    key_projection_weight,
    value_projection_weight,
    w_out,
    mlp_norm,
    w_gate,
    w_up,
    w_down,
):
    batch_count, row_count, local_width = tokens.shape
    group_size = SEQUENCE_LENGTH // row_count
    stride = lax.axis_size("fsdp") // group_size
    head_count = w_query.shape[1] // HEAD_SIZE
    score_scale = HEAD_SIZE ** (-0.5)
    local_rank = lax.axis_index("fsdp") // stride
    row_ids = jnp.arange(row_count, dtype=jnp.int32)
    query_index = local_rank * row_count + row_ids
    column_start = lax.axis_index("tp") * local_width
    accumulated = None
    outputs = []
    input_grads = []
    for batch in range(batch_count):
        attn_full = (
            lax.all_gather(attn_norm, "fsdp", axis=0, tiled=True),
            lax.all_gather(w_query, "fsdp", axis=0, tiled=True),
            lax.all_gather(key_projection_weight, "fsdp", axis=0, tiled=True),
            lax.all_gather(value_projection_weight, "fsdp", axis=0, tiled=True),
            lax.all_gather(w_out, "fsdp", axis=1, tiled=True),
        )
        mlp_full = (
            lax.all_gather(mlp_norm, "fsdp", axis=0, tiled=True),
            lax.all_gather(w_gate, "fsdp", axis=0, tiled=True),
            lax.all_gather(w_up, "fsdp", axis=0, tiled=True),
            lax.all_gather(w_down, "fsdp", axis=1, tiled=True),
        )
        if accumulated is None:
            accumulated = [
                jnp.zeros(attn_full[0].shape, jnp.float32),
                jnp.zeros(attn_full[1].shape, jnp.float32),
                jnp.zeros(attn_full[2].shape, jnp.float32),
                jnp.zeros(attn_full[3].shape, jnp.float32),
                jnp.zeros(attn_full[4].shape, jnp.float32),
                jnp.zeros(mlp_full[0].shape, jnp.float32),
                jnp.zeros(mlp_full[1].shape, jnp.float32),
                jnp.zeros(mlp_full[2].shape, jnp.float32),
                jnp.zeros(mlp_full[3].shape, jnp.float32),
            ]
        gain_one = attn_full[0].astype(jnp.float32)
        query_weight, key_weight, value_weight, out_weight = (
            attn_full[1],
            attn_full[2],
            attn_full[3],
            attn_full[4],
        )
        gain_two = mlp_full[0].astype(jnp.float32)
        gate_weight, up_weight, down_weight = (mlp_full[1], mlp_full[2], mlp_full[3])
        local_in = tokens[batch]
        input_low = full_width(local_in)
        input_float = input_low.astype(jnp.float32)
        scale_one = lax.rsqrt(jnp.mean(input_float * input_float, -1, keepdims=True) + NORM_EPSILON)
        normed_one = (input_float * scale_one * gain_one).astype(jnp.bfloat16)
        query = jnp.dot(normed_one, query_weight, preferred_element_type=jnp.float32)
        key_projected = jnp.dot(normed_one, key_weight, preferred_element_type=jnp.float32)
        value_projected = jnp.dot(normed_one, value_weight, preferred_element_type=jnp.float32)
        cosine_table, sine_lookup = rope_tables(positions[batch], HEAD_SIZE)
        query_rotated = apply_rotary(
            query.reshape(row_count, head_count, HEAD_SIZE), cosine_table, sine_lookup
        ).astype(jnp.bfloat16)
        key_rotated = apply_rotary(
            key_projected.reshape(row_count, 1, HEAD_SIZE), cosine_table, sine_lookup
        )[:, 0].astype(jnp.bfloat16)
        value_narrow = value_projected.astype(jnp.bfloat16)
        segment_low = segment_ids[batch].astype(jnp.bfloat16)
        key_blocks = [(key_rotated, value_narrow, segment_low, query_index, local_rank >= 0)]
        for offset in range(1, group_size):
            moved_keys, moved_values, moved_segments = passed_along(
                (key_rotated, value_narrow, segment_low), "fsdp", offset * stride
            )
            key_blocks.append(
                (
                    moved_keys,
                    moved_values,
                    moved_segments,
                    (local_rank - offset) * row_count + row_ids,
                    offset <= local_rank,
                )
            )
        heads_low, log_total = attend_forward(
            query_rotated, key_blocks, segment_low, query_index, score_scale
        )
        heads_out = heads_low.reshape(row_count, head_count * HEAD_SIZE)
        attn_own = width_sum(jnp.dot(heads_out, out_weight, preferred_element_type=jnp.float32))
        middle_own = local_in.astype(jnp.float32) + attn_own
        middle = lax.all_gather(middle_own, "tp", axis=1, tiled=True)
        scale_two = lax.rsqrt(jnp.mean(middle * middle, -1, keepdims=True) + NORM_EPSILON)
        normed_two = (middle * scale_two * gain_two).astype(jnp.bfloat16)
        gate = jnp.dot(normed_two, gate_weight, preferred_element_type=jnp.float32)
        up_proj = jnp.dot(normed_two, up_weight, preferred_element_type=jnp.float32)
        sigmoid_gate = jax.nn.sigmoid(gate)
        activated = (gate * sigmoid_gate * up_proj).astype(jnp.bfloat16)
        mlp_own = width_sum(jnp.dot(activated, down_weight, preferred_element_type=jnp.float32))
        outputs.append((middle_own + mlp_own).astype(jnp.bfloat16))
        mlp_back = (
            lax.all_gather(mlp_norm, "fsdp", axis=0, tiled=True),
            lax.all_gather(w_gate, "fsdp", axis=0, tiled=True),
            lax.all_gather(w_up, "fsdp", axis=0, tiled=True),
            lax.all_gather(w_down, "fsdp", axis=1, tiled=True),
        )
        back_gain_two = mlp_back[0].astype(jnp.float32)
        grad_low = full_width(out_grad[batch])
        accumulated[8] = accumulated[8] + outer_sum(activated, grad_low)
        grad_act = transposed_product(grad_low, mlp_back[3])
        grad_gate_low = (
            grad_act * up_proj * sigmoid_gate * (1.0 + gate * (1.0 - sigmoid_gate))
        ).astype(jnp.bfloat16)
        grad_up_low = (grad_act * gate * sigmoid_gate).astype(jnp.bfloat16)
        accumulated[6] = accumulated[6] + outer_sum(normed_two, grad_gate_low)
        accumulated[7] = accumulated[7] + outer_sum(normed_two, grad_up_low)
        grad_normed_two = back_sum(
            transposed_product(grad_gate_low, mlp_back[1])
            + transposed_product(grad_up_low, mlp_back[2])
        )
        accumulated[5] = accumulated[5] + jnp.sum(grad_normed_two * middle * scale_two, 0)
        scaled_two = grad_normed_two * back_gain_two
        grad_middle = (
            grad_low.astype(jnp.float32)
            + scale_two * scaled_two
            - middle
            * (scale_two * scale_two * scale_two)
            * jnp.mean(scaled_two * middle, -1, keepdims=True)
        )
        middle_low = grad_middle.astype(jnp.bfloat16)
        attn_back = (
            lax.all_gather(attn_norm, "fsdp", axis=0, tiled=True),
            lax.all_gather(w_query, "fsdp", axis=0, tiled=True),
            lax.all_gather(key_projection_weight, "fsdp", axis=0, tiled=True),
            lax.all_gather(value_projection_weight, "fsdp", axis=0, tiled=True),
            lax.all_gather(w_out, "fsdp", axis=1, tiled=True),
        )
        back_gain_one = attn_back[0].astype(jnp.float32)
        accumulated[4] = accumulated[4] + outer_sum(heads_out, middle_low)
        gradient_by_head = (
            transposed_product(middle_low, attn_back[4])
            .astype(jnp.bfloat16)
            .reshape(row_count, head_count, HEAD_SIZE)
        )
        grad_query_rot, block_grads = attend_backward(
            query_rotated,
            key_blocks,
            segment_low,
            query_index,
            log_total,
            heads_low,
            gradient_by_head,
            score_scale,
        )
        own_keys, own_values = block_grads[0]
        for offset in range(1, group_size):
            back_keys, back_values = passed_along(
                (block_grads[offset][0], block_grads[offset][1]), "fsdp", -offset * stride
            )
            own_keys = own_keys + back_keys
            own_values = own_values + back_values
        grad_query_low = (
            reverse_rotary(grad_query_rot, cosine_table, sine_lookup)
            .reshape(row_count, head_count * HEAD_SIZE)
            .astype(jnp.bfloat16)
        )
        key_gradient_narrow = reverse_rotary(own_keys[:, None, :], cosine_table, sine_lookup)[
            :, 0
        ].astype(jnp.bfloat16)
        value_gradient_narrow = own_values.astype(jnp.bfloat16)
        accumulated[1] = accumulated[1] + outer_sum(normed_one, grad_query_low)
        accumulated[2] = accumulated[2] + outer_sum(normed_one, key_gradient_narrow)
        accumulated[3] = accumulated[3] + outer_sum(normed_one, value_gradient_narrow)
        grad_normed_one = back_sum(
            transposed_product(grad_query_low, attn_back[1])
            + transposed_product(key_gradient_narrow, attn_back[2])
            + transposed_product(value_gradient_narrow, attn_back[3])
        )
        accumulated[0] = accumulated[0] + jnp.sum(grad_normed_one * input_float * scale_one, 0)
        scaled_one = grad_normed_one * back_gain_one
        input_grad = (
            grad_middle
            + scale_one * scaled_one
            - input_float
            * (scale_one * scale_one * scale_one)
            * jnp.mean(scaled_one * input_float, -1, keepdims=True)
        )
        input_grads.append(lax.dynamic_slice_in_dim(input_grad, column_start, local_width, 1))
    summed = (
        lax.psum_scatter(accumulated[0], "fsdp", scatter_dimension=0, tiled=True),
        lax.psum_scatter(accumulated[1], "fsdp", scatter_dimension=0, tiled=True),
        lax.psum_scatter(accumulated[2], "fsdp", scatter_dimension=0, tiled=True),
        lax.psum_scatter(accumulated[3], "fsdp", scatter_dimension=0, tiled=True),
        lax.psum_scatter(accumulated[4], "fsdp", scatter_dimension=1, tiled=True),
        lax.psum_scatter(accumulated[5], "fsdp", scatter_dimension=0, tiled=True),
        lax.psum_scatter(accumulated[6], "fsdp", scatter_dimension=0, tiled=True),
        lax.psum_scatter(accumulated[7], "fsdp", scatter_dimension=0, tiled=True),
        lax.psum_scatter(accumulated[8], "fsdp", scatter_dimension=1, tiled=True),
    )
    grad_scale = (batch_count * row_count * lax.axis_size("fsdp")) ** (-0.5)
    return (
        jnp.stack(outputs),
        jnp.stack(input_grads),
        summed[0] * grad_scale,
        summed[1] * grad_scale,
        summed[2] * grad_scale,
        summed[3] * grad_scale,
        summed[4] * grad_scale,
        summed[5] * grad_scale,
        summed[6] * grad_scale,
        summed[7] * grad_scale,
        summed[8] * grad_scale,
    )


def solution(mesh):
    in_specs = (
        P(None, "fsdp", "tp"),
        P(None, "fsdp", "tp"),
        P(None, "fsdp"),
        P(None, "fsdp"),
        P("fsdp"),
        P("fsdp", "tp"),
        P("fsdp", "tp"),
        P("fsdp", "tp"),
        P("tp", "fsdp"),
        P("fsdp"),
        P("fsdp", "tp"),
        P("fsdp", "tp"),
        P("tp", "fsdp"),
    )
    out_specs = (
        P(None, "fsdp", "tp"),
        P(None, "fsdp", "tp"),
        P("fsdp"),
        P("fsdp", "tp"),
        P("fsdp", "tp"),
        P("fsdp", "tp"),
        P("tp", "fsdp"),
        P("fsdp"),
        P("fsdp", "tp"),
        P("fsdp", "tp"),
        P("tp", "fsdp"),
    )
    return jax.shard_map(shards, mesh=mesh, in_specs=in_specs, out_specs=out_specs, check_vma=False)
```

profile of v0, /device:TPU:0, one launch (start us, length us, event | category | flops | bytes accessed | tf_op | source)
XLA Modules:
  0.0 1453.3 jit_solution(836459257052332692)
XLA Ops:
  22.0 8.3 all_gather.32
  30.3 9.5 all-gather.4
  39.9 8.7 all_gather.33
  94.9 6.7 all-gather.18.cloned.1.call-done
  201.9 45.0 %reduce-scatter.16.cloned.1.call-done = f32[256,512]{1,0:T(8,128)} async-done(((f32[256,2048]{1,0:T(8,128)}), f32[256,512]{1,0:T(8,128)}) %reduce-scatter.16.cloned.1.call-update) | async-done | bytes 524304 | tf_op jit(solution)/shard_map/reduce_scatter | solution.py:61
  253.6 9.1 all-gather.5
  262.7 31.6 %all-gather.22.cloned.1.call-done = f32[256,2048]{1,0:T(8,128)} async-done(((f32[256,512]{1,0:T(8,128)}), f32[256,2048]{1,0:T(8,128)}) %all-gather.22.cloned.1.call-update) | async-done | bytes 2097168 | tf_op jit(solution)/shard_map/all_gather | solution.py:244
  296.2 44.7 %all-gather.30.cloned.1.call-done = f32[256,2048]{1,0:T(8,128)} async-done(((f32[256,512]{1,0:T(8,128)}), f32[256,2048]{1,0:T(8,128)}) %all-gather.30.cloned.1.call-update) | async-done | bytes 2097168 | tf_op jit(solution)/shard_map/all_gather | solution.py:244
  344.8 40.0 %all-gather.24.cloned.1.call-done = bf16[2048,1408]{1,0:T(8,128)(2,1)} async-done(((bf16[256,1408]{1,0:T(8,128)(2,1)}), bf16[2048,1408]{1,0:T(8,128)(2,1)}) %all-gather.24.cloned.1.call-update) | async-done | bytes 5767184 | tf_op jit(solution)/shard_map/all_gather | solution.py:182
  390.7 39.1 %all-gather.26.cloned.1.call-done = bf16[2048,1408]{1,0:T(8,128)(2,1)} async-done(((bf16[256,1408]{1,0:T(8,128)(2,1)}), bf16[2048,1408]{1,0:T(8,128)(2,1)}) %all-gather.26.cloned.1.call-update) | async-done | bytes 5767184 | tf_op jit(solution)/shard_map/all_gather | solution.py:183
  435.6 23.7 %all-gather.38.cloned.1.call-done = bf16[1,256,2048]{2,1,0:T(8,128)(2,1)} async-done(((bf16[1,256,512]{2,1,0:T(8,128)(2,1)}), bf16[1,256,2048]{2,1,0:T(8,128)(2,1)}) %all-gather.38.cloned.1.call-update) | async-done | bytes 1048592 | tf_op jit(solution)/shard_map/all_gather | solution.py:57
  459.3 45.4 %all-gather.28.cloned.1.call-done = bf16[1408,2048]{1,0:T(8,128)(2,1)} async-done(((bf16[1408,256]{1,0:T(8,128)(2,1)}), bf16[1408,2048]{1,0:T(8,128)(2,1)}) %all-gather.28.cloned.1.call-update) | async-done | bytes 5767184 | tf_op jit(solution)/shard_map/all_gather | solution.py:184
  504.7 7.4 multiply_convert_fusion.2
  521.1 13.7 all-gather.36.cloned.1.call-done
  534.9 7.0 multiply_convert_fusion.4
  568.6 142.3 %all-reduce.10.cloned.1.call-done = (f32[256,2048]{1,0:T(8,128)}, f32[256,2048]{1,0:T(8,128)}) async-done(((f32[256,2048]{1,0:T(8,128)}, f32[256,2048]{1,0:T(8,128)}), (f32[256,2048]{1,0:T(8,128)}, f32[256,2048]{1,0:T(8,128)})) %all-reduce.10.cloned.1.call-update) | async-done | bytes 4194320 | tf_op jit(solution)/shard_map/psum | solution.py:65
  881.4 6.2 convolution_add_fusion.1
  909.8 154.6 %all-reduce.8.cloned.1.call-done = (f32[256,2048]{1,0:T(8,128)}, f32[256,2048]{1,0:T(8,128)}) async-done(((f32[256,2048]{1,0:T(8,128)}, f32[256,2048]{1,0:T(8,128)}), (f32[256,2048]{1,0:T(8,128)}, f32[256,2048]{1,0:T(8,128)})) %all-reduce.8.cloned.1.call-update) | async-done | bytes 4194320 | tf_op jit(solution)/shard_map/psum | solution.py:65
  1069.5 24.0 %all-reduce.2 = (f32[2048]{0:T(1024)S(1)}, f32[2048]{0:T(1024)S(1)}) all-reduce(f32[2048]{0:T(1024)S(1)} %add.748, f32[2048]{0:T(1024)S(1)} %add.753), channel_id=10, replica_groups=mesh['fsdp'=8,'tp'=4] {'fsdp'}, use_global_device_ids=true, to_apply=%region_52.53.clone | all-reduce | flops 4096 | bytes 32768
  1098.8 18.9 %reduce-scatter.20.cloned.1.call-done = f32[256,512]{1,0:T(8,128)} async-done(((f32[2048,512]{1,0:T(8,128)}), f32[256,512]{1,0:T(8,128)}) %reduce-scatter.20.cloned.1.call-update) | async-done | bytes 524304 | tf_op jit(solution)/shard_map/reduce_scatter | solution.py:343
  1119.6 52.6 %reduce-scatter.26.cloned.1.call-done = f32[512,256]{1,0:T(8,128)} async-done(((f32[512,2048]{1,0:T(8,128)}), f32[512,256]{1,0:T(8,128)}) %reduce-scatter.26.cloned.1.call-update) | async-done | bytes 524304 | tf_op jit(solution)/shard_map/reduce_scatter | solution.py:346
  1174.1 88.8 %reduce-scatter.28.cloned.1.call-done = f32[256,1408]{1,0:T(8,128)} async-done(((f32[2048,1408]{1,0:T(8,128)}), f32[256,1408]{1,0:T(8,128)}) %reduce-scatter.28.cloned.1.call-update) | async-done | bytes 1441808 | tf_op jit(solution)/shard_map/reduce_scatter | solution.py:348
  1265.4 88.1 %reduce-scatter.30.cloned.1.call-done = f32[256,1408]{1,0:T(8,128)} async-done(((f32[2048,1408]{1,0:T(8,128)}), f32[256,1408]{1,0:T(8,128)}) %reduce-scatter.30.cloned.1.call-update) | async-done | bytes 1441808 | tf_op jit(solution)/shard_map/reduce_scatter | solution.py:349
  1356.1 87.7 %reduce-scatter.32.cloned.1.call-done = f32[1408,256]{1,0:T(8,128)} async-done(((f32[1408,2048]{1,0:T(8,128)}), f32[1408,256]{1,0:T(8,128)}) %reduce-scatter.32.cloned.1.call-update) | async-done | bytes 1441808 | tf_op jit(solution)/shard_map/reduce_scatter | solution.py:350
  (880 shorter events, 431.2 us)
Async XLA Ops:
  7.2 63.4 %all-gather.32.cloned.1.call-start = ((), (), s32[]{:S(2)}) async-start(), calls=%async_computation.29 | async-start | bytes 1310720 | tf_op jit(solution)/shard_map/all_gather | solution.py:57
  9.1 76.8 %all-gather.34.cloned.1.call-start = ((), (), s32[]{:S(2)}) async-start(), calls=%async_computation.30 | async-start | bytes 1310720 | tf_op jit(solution)/shard_map/all_gather | solution.py:57
  9.9 91.8 %all-gather.18.cloned.1.call-start = ((), (), s32[]{:S(2)}) async-start(), calls=%async_computation.11 | async-start | bytes 2359296 | tf_op jit(solution)/shard_map/all_gather | solution.py:175
  10.6 144.5 %all-gather.20.cloned.1.call-start = ((), (), s32[]{:S(2)}) async-start(), calls=%async_computation.12 | async-start | bytes 2359296 | tf_op jit(solution)/shard_map/all_gather | solution.py:178
  21.9 179.9 %reduce-scatter.12.cloned.1.call-start = ((), (), s32[]{:S(2)}) async-start(), calls=%async_computation.13 | async-start | bytes 2621440 | tf_op jit(solution)/shard_map/reduce_scatter | solution.py:61
  158.9 87.9 %reduce-scatter.16.cloned.1.call-start = ((), (), s32[]{:S(2)}) async-start(), calls=%async_computation.19 | async-start | bytes 2621440 | tf_op jit(solution)/shard_map/reduce_scatter | solution.py:61
  196.4 97.9 %all-gather.22.cloned.1.call-start = ((), (), s32[]{:S(2)}) async-start(), calls=%async_computation.14 | async-start | bytes 2621440 | tf_op jit(solution)/shard_map/all_gather | solution.py:244
  249.2 91.7 %all-gather.30.cloned.1.call-start = ((), (), s32[]{:S(2)}) async-start(), calls=%async_computation.20 | async-start | bytes 2621440 | tf_op jit(solution)/shard_map/all_gather | solution.py:244
  250.0 134.8 %all-gather.24.cloned.1.call-start = ((), (), s32[]{:S(2)}) async-start(), calls=%async_computation.15 | async-start | bytes 6488064 | tf_op jit(solution)/shard_map/all_gather | solution.py:182
  250.7 179.0 %all-gather.26.cloned.1.call-start = ((), (), s32[]{:S(2)}) async-start(), calls=%async_computation.16 | async-start | bytes 6488064 | tf_op jit(solution)/shard_map/all_gather | solution.py:183
  251.3 208.0 %all-gather.38.cloned.1.call-start = ((), (), s32[]{:S(2)}) async-start(), calls=%async_computation.32 | async-start | bytes 1310720 | tf_op jit(solution)/shard_map/all_gather | solution.py:57
  252.2 252.5 %all-gather.28.cloned.1.call-start = ((), (), s32[]{:S(2)}) async-start(), calls=%async_computation.17 | async-start | bytes 6488064 | tf_op jit(solution)/shard_map/all_gather | solution.py:184
  252.8 282.1 %all-gather.36.cloned.1.call-start = ((), (), s32[]{:S(2)}) async-start(), calls=%async_computation.31 | async-start | bytes 1310720 | tf_op jit(solution)/shard_map/all_gather | solution.py:57
  253.5 457.5 %all-reduce.10.cloned.1.call-start = ((), (), s32[]{:S(2)}) async-start(), calls=%async_computation.34 | async-start | bytes 8388608 | tf_op jit(solution)/shard_map/psum | solution.py:65
  556.5 347.0 %reduce-scatter.18.cloned.1.call-start = ((), (), s32[]{:S(2)}) async-start(), calls=%async_computation.21 | async-start | bytes 2621440 | tf_op jit(solution)/shard_map/reduce_scatter | solution.py:61
  562.5 342.2 %reduce-scatter.14.cloned.1.call-start = ((), (), s32[]{:S(2)}) async-start(), calls=%async_computation.18 | async-start | bytes 2621440 | tf_op jit(solution)/shard_map/reduce_scatter | solution.py:61
  568.6 338.3 %reduce-scatter.22.cloned.1.call-start = ((), (), s32[]{:S(2)}) async-start(), calls=%async_computation.23 | async-start | bytes 589824 | tf_op jit(solution)/shard_map/reduce_scatter | solution.py:344
  830.8 77.6 %reduce-scatter.24.cloned.1.call-start = ((), (), s32[]{:S(2)}) async-start(), calls=%async_computation.24 | async-start | bytes 589824 | tf_op jit(solution)/shard_map/reduce_scatter | solution.py:345
  850.5 213.9 %all-reduce.8.cloned.1.call-start = ((), (), s32[]{:S(2)}) async-start(), calls=%async_computation.33 | async-start | bytes 8388608 | tf_op jit(solution)/shard_map/psum | solution.py:65
  856.5 261.3 %reduce-scatter.20.cloned.1.call-start = ((), (), s32[]{:S(2)}) async-start(), calls=%async_computation.22 | async-start | bytes 4718592 | tf_op jit(solution)/shard_map/reduce_scatter | solution.py:343
  862.0 310.3 %reduce-scatter.26.cloned.1.call-start = ((), (), s32[]{:S(2)}) async-start(), calls=%async_computation.25 | async-start | bytes 4718592 | tf_op jit(solution)/shard_map/reduce_scatter | solution.py:346
  868.2 394.6 %reduce-scatter.28.cloned.1.call-start = ((), (), s32[]{:S(2)}) async-start(), calls=%async_computation.26 | async-start | bytes 12976128 | tf_op jit(solution)/shard_map/reduce_scatter | solution.py:348
  877.9 475.6 %reduce-scatter.30.cloned.1.call-start = ((), (), s32[]{:S(2)}) async-start(), calls=%async_computation.27 | async-start | bytes 12976128 | tf_op jit(solution)/shard_map/reduce_scatter | solution.py:349
  887.6 556.2 %reduce-scatter.32.cloned.1.call-start = ((), (), s32[]{:S(2)}) async-start(), calls=%async_computation.28 | async-start | bytes 12976128 | tf_op jit(solution)/shard_map/reduce_scatter | solution.py:350
  (292 other events, 3278.9 us)
Sparse Core Ops, SparseCore 0:
  10.2 30.6 all-gather.31
  43.0 27.3 all-gather.33
  72.3 29.2 all-gather.17
  103.4 28.1 all-gather.19
  159.1 42.7 reduce-scatter.11
  204.0 42.8 reduce-scatter.15
  249.3 44.8 all-gather.21
  296.4 44.4 all-gather.29
  342.8 41.9 all-gather.23
  386.5 43.1 all-gather.25
  431.3 27.9 all-gather.37
  461.1 43.6 all-gather.27
  506.9 27.9 all-gather.35
  556.6 154.3 all-reduce.9
  713.1 42.5 reduce-scatter.17
  757.9 42.8 reduce-scatter.13
  830.9 38.8 reduce-scatter.21
  872.8 34.1 reduce-scatter.23
  909.4 154.9 all-reduce.7
  1067.6 50.1 reduce-scatter.19
  1121.1 51.0 reduce-scatter.25
  1175.7 87.1 reduce-scatter.27
  1266.4 87.1 reduce-scatter.29
  1356.9 86.8 reduce-scatter.31
where the time goes:
time: 1470 us; the launch traced here: 1450 us
  waiting for transfers between devices  940 us (64%)
  matrix products  221 us (15%)
  starting transfers between devices  117 us (8%)
  other arithmetic  70.2 us (5%)
  blocking collectives  59.6 us (4%)
  local copies, waits for them, and re-layouts  26.4 us (2%)
  between operations  19.2 us (1%)
    psum x2, waiting for transfers between devices, back_sum(): return lax.psum(partial_term, 'tp')  297 us
    ppermute x70, starting transfers between devices, passed_along(): return lax.ppermute(block, axis, route)  115 us
    reduce_scatter x1, waiting for transfers between devices, shards(): lax.psum_scatter(accumulated[6], 'fsdp', scatter_dimension=0, tiled=True)  88.8 us
    reduce_scatter x1, waiting for transfers between devices, shards(): lax.psum_scatter(accumulated[7], 'fsdp', scatter_dimension=0, tiled=True)  88.1 us
    reduce_scatter x1, waiting for transfers between devices, shards(): lax.psum_scatter(accumulated[8], 'fsdp', scatter_dimension=1, tiled=True)  87.7 us
    all_gather x2, waiting for transfers between devices, shards(): middle = lax.all_gather(middle_own, 'tp', axis=1, tiled=True)  76.2 us
    reduce_scatter x1, waiting for transfers between devices, shards(): lax.psum_scatter(accumulated[4], 'fsdp', scatter_dimension=1, tiled=True)  52.6 us
    reduce_scatter x4, waiting for transfers between devices, width_sum(): return lax.psum_scatter(partial_term, 'tp', scatter_dimension=1, tiled=True)  50.5 us
  transfers between devices with their start and end apart: 94, of which 24 were waited for; matrix products, arithmetic and copies ran while one was open for 19% of the time, Pallas kernels for 0%

commit v1 on v0

v1 whole, which is shorter than its diff:
```python
import jax
import jax.numpy as jnp
from jax import lax
from jax.sharding import PartitionSpec as P

HEAD_SIZE = 64
SEQUENCE_LENGTH = 2048
DOC_MAX = 1024


NORM_EPSILON = 1e-05
ROPE_BASE = 10000.0
MASKED_SCORE = -1e30
GAIN_COLUMNS = 128

F32 = jnp.float32
BF16 = jnp.bfloat16


def rope_tables(offsets, head_width):
    half_width = head_width // 2
    inverse = ROPE_BASE ** (-(jnp.arange(half_width, dtype=F32) * 2.0 / head_width))
    angles = offsets.astype(F32)[:, None] * inverse[None, :]
    cosine_table = jnp.concatenate([jnp.cos(angles), jnp.cos(angles)], -1)
    sine_lookup = jnp.concatenate([jnp.sin(angles), jnp.sin(angles)], -1)
    return (cosine_table, sine_lookup)


def apply_rotary(vectors, cosine_table, sine_lookup):
    half_width = vectors.shape[-1] // 2
    turned = jnp.concatenate([-vectors[..., half_width:], vectors[..., :half_width]], -1)
    return vectors * cosine_table[:, None, :] + turned * sine_lookup[:, None, :]


def reverse_rotary(cotangent, cosine_table, sine_lookup):
    half_width = cotangent.shape[-1] // 2
    scaled = cotangent * sine_lookup[:, None, :]
    return cotangent * cosine_table[:, None, :] + jnp.concatenate(
        [scaled[..., half_width:], -scaled[..., :half_width]], -1
    )


def dot_nn(left, right):
    return jnp.dot(left, right, preferred_element_type=F32)


def dot_nt(left, right):
    return lax.dot_general(left, right, (((1,), (1,)), ((), ())), preferred_element_type=F32)


def dot_tn(left, right):
    return lax.dot_general(left, right, (((0,), (0,)), ((), ())), preferred_element_type=F32)


def exchange(block, axis, mask):
    return lax.ppermute(block, axis, [(i, i ^ mask) for i in range(lax.axis_size(axis))])


def passed_along(block, axis, distance):
    devices = range(lax.axis_size(axis))
    route = [(i - distance, i) for i in devices if i - distance in devices]
    return lax.ppermute(block, axis, route)


def tp_gather(part):
    size = lax.axis_size("tp")
    index = lax.axis_index("tp")
    held = part[None]
    bit = size // 2
    order = []
    while bit:
        other = exchange(held, "tp", bit)
        mine_first = (index & bit) == 0
        held = jnp.where(
            mine_first, jnp.stack([held, other]), jnp.stack([other, held])
        )
        order.append(bit)
        bit //= 2
    held = held.reshape((2,) * len(order) + part.shape)
    axes = tuple(reversed(range(len(order))))
    held = held.transpose((len(order),) + axes + (len(order) + 1,))
    return held.reshape(part.shape[0], size * part.shape[1])


def tp_scatter_sum(partial):
    size = lax.axis_size("tp")
    index = lax.axis_index("tp")
    rows, full = partial.shape
    held = partial.reshape(rows, size, full // size)
    bit = 1
    slots = size
    while bit < size:
        split = held.reshape(rows, slots // 2, 2, full // size)
        low = (index & bit) == 0
        keep = jnp.where(low, split[:, :, 0], split[:, :, 1])
        send = jnp.where(low, split[:, :, 1], split[:, :, 0]).astype(BF16)
        held = keep + exchange(send, "tp", bit).astype(F32)
        slots //= 2
        bit *= 2
    return held.reshape(rows, full // size)


def queue_gather(part):
    return lax.all_gather(part, "tp", axis=1, tiled=True)


def queue_scatter_sum(partial):
    return lax.psum_scatter(partial.astype(BF16), "tp", scatter_dimension=1, tiled=True)


def owner_block(array, owner, axis):
    width = array.shape[axis] // lax.axis_size("fsdp")
    return lax.dynamic_slice_in_dim(array, owner * width, width, axis)


def owner_sums(block_of):
    size = lax.axis_size("fsdp")
    index = lax.axis_index("fsdp")
    pairs = size // 2
    away = jnp.stack([block_of((index ^ 1) ^ (2 * m)).astype(BF16) for m in range(pairs)])
    other = exchange(away, "fsdp", 1)
    total = None
    for m in reversed(range(pairs)):
        term = block_of(index ^ (2 * m)) + other[m].astype(F32)
        if m:
            term = exchange(term.astype(BF16), "fsdp", 2 * m).astype(F32)
        total = term if total is None else total + term
    return total


def allowed_keys(offsets, row_count, back):
    row = jnp.arange(row_count, dtype=jnp.int32)[:, None] + back * row_count
    first = row - offsets[:, None]
    key = jnp.arange((back + 1) * row_count, dtype=jnp.int32)[None, :]
    return ((key >= first) & (key <= row))[None]


def attend_forward(query_rotated, keys, values, allowed, score_scale):
    scores = (
        jnp.einsum("lhd,md->hlm", query_rotated, keys, preferred_element_type=F32) * score_scale
    )
    scores = jnp.where(allowed, scores, MASKED_SCORE)
    row_max = jnp.max(scores, -1)
    row_sum = jnp.sum(jnp.where(allowed, jnp.exp(scores - row_max[..., None]), 0.0), -1)
    log_total = row_max + jnp.log(row_sum)
    prob_round = jnp.where(allowed, jnp.exp(scores - log_total[..., None]), 0.0).astype(BF16)
    heads = jnp.einsum("hlm,md->lhd", prob_round, values, preferred_element_type=F32)
    return (heads.astype(BF16), log_total)


def attend_backward(
    query_rotated, keys, values, allowed, log_total, heads_low, grad_low, score_scale
):
    delta = jnp.sum(grad_low.astype(F32) * heads_low.astype(F32), -1).T
    scores = (
        jnp.einsum("lhd,md->hlm", query_rotated, keys, preferred_element_type=F32) * score_scale
    )
    prob_exact = jnp.where(allowed, jnp.exp(scores - log_total[..., None]), 0.0)
    prob_round = prob_exact.astype(BF16)
    grad_values = jnp.einsum("hlm,lhd->md", prob_round, grad_low, preferred_element_type=F32)
    grad_probs = jnp.einsum("lhd,md->hlm", grad_low, values, preferred_element_type=F32)
    grad_scores = (prob_exact * (grad_probs - delta[..., None]) * score_scale).astype(BF16)
    grad_query = jnp.einsum("hlm,md->lhd", grad_scores, keys, preferred_element_type=F32)
    grad_keys = jnp.einsum("hlm,lhd->md", grad_scores, query_rotated, preferred_element_type=F32)
    return (grad_query, grad_keys, grad_values)


def shards(
    tokens,
    out_grad,
    segment_ids,
    positions,
    attn_norm,
    w_query,
    key_projection_weight,
    value_projection_weight,
    w_out,
    mlp_norm,
    w_gate,
    w_up,
    w_down,
):
    batch_count, row_count, local_width = tokens.shape
    batches = range(batch_count)
    full_width = local_width * lax.axis_size("tp")
    group_size = SEQUENCE_LENGTH // row_count
    stride = lax.axis_size("fsdp") // group_size
    query_width = w_query.shape[1]
    hidden = w_gate.shape[1]
    head_count = query_width // HEAD_SIZE
    score_scale = HEAD_SIZE ** (-0.5)
    back = min(group_size - 1, -(-(DOC_MAX - 1) // row_count))
    column_start = lax.axis_index("tp") * local_width
    shard_rows = w_query.shape[0]

    gains = jnp.stack([attn_norm, mlp_norm], 1)
    gains = jnp.pad(gains, ((0, 0), (0, GAIN_COLUMNS - 2)))
    first_shard = jnp.concatenate(
        [w_query, key_projection_weight, value_projection_weight, gains], 1
    )
    first_full = lax.all_gather(first_shard, "fsdp", axis=0, tiled=True)
    project_width = query_width + 2 * HEAD_SIZE
    project_weight = first_full[:, :project_width]
    gain_rows = first_full[:, project_width : project_width + 2].astype(F32).T
    gain_one, gain_two = gain_rows[0], gain_rows[1]
    out_weight = lax.all_gather(w_out, "fsdp", axis=1, tiled=True)
    gate_up_weight = lax.all_gather(
        jnp.concatenate([w_gate, w_up], 1), "fsdp", axis=0, tiled=True
    )
    down_weight = lax.all_gather(w_down, "fsdp", axis=1, tiled=True)

    inputs = [tp_gather(tokens[b]).astype(F32) for b in batches]
    scale_one = [
        lax.rsqrt(jnp.mean(x * x, -1, keepdims=True) + NORM_EPSILON) for x in inputs
    ]
    normed_one = jnp.concatenate(
        [(inputs[b] * scale_one[b] * gain_one).astype(BF16) for b in batches], 0
    )
    projected = dot_nn(normed_one, project_weight)
    cosine_table, sine_lookup = rope_tables(positions.reshape(-1), HEAD_SIZE)
    query_rotated = apply_rotary(
        projected[:, :query_width].reshape(-1, head_count, HEAD_SIZE), cosine_table, sine_lookup
    ).astype(BF16)
    key_rotated = apply_rotary(
        projected[:, None, query_width : query_width + HEAD_SIZE], cosine_table, sine_lookup
    )[:, 0].astype(BF16)
    pairs = jnp.concatenate(
        [key_rotated, projected[:, query_width + HEAD_SIZE :].astype(BF16)], -1
    ).reshape(batch_count, row_count, 2 * HEAD_SIZE)
    window = [passed_along(pairs, "fsdp", o * stride) for o in range(back, 0, -1)] + [pairs]
    window = jnp.concatenate(window, 1)
    keys, values = window[..., :HEAD_SIZE], window[..., HEAD_SIZE:]

    cut = lambda array, b: array[b * row_count : (b + 1) * row_count]
    grads_in = [queue_gather(out_grad[b]) for b in batches]
    allowed, heads, totals, middle_own, middle = [], [], [], [], []
    for b in batches:
        allowed.append(allowed_keys(positions[b], row_count, back))
        heads_b, total_b = attend_forward(
            cut(query_rotated, b), keys[b], values[b], allowed[b], score_scale
        )
        heads.append(heads_b)
        totals.append(total_b)
        attn_own = tp_scatter_sum(dot_nn(heads_b.reshape(row_count, query_width), out_weight))
        middle_own.append(tokens[b].astype(F32) + attn_own)
        middle.append(tp_gather(middle_own[b].astype(BF16)).astype(F32))

    outputs, scale_two, normed_two, activated, grad_pair, grad_normed_two = [], [], [], [], [], []
    for b in batches:
        scale_two.append(
            lax.rsqrt(jnp.mean(middle[b] * middle[b], -1, keepdims=True) + NORM_EPSILON)
        )
        normed_two.append((middle[b] * scale_two[b] * gain_two).astype(BF16))
        both = dot_nn(normed_two[b], gate_up_weight)
        gate, up_proj = both[:, :hidden], both[:, hidden:]
        sigmoid_gate = jax.nn.sigmoid(gate)
        activated.append((gate * sigmoid_gate * up_proj).astype(BF16))
        grad_act = dot_nn(grads_in[b], down_weight.T)
        grad_gate_low = (
            grad_act * up_proj * sigmoid_gate * (1.0 + gate * (1.0 - sigmoid_gate))
        ).astype(BF16)
        grad_up_low = (grad_act * gate * sigmoid_gate).astype(BF16)
        grad_pair.append(jnp.concatenate([grad_gate_low, grad_up_low], 1))
        grad_normed_two.append(
            queue_gather(queue_scatter_sum(dot_nt(grad_pair[b], gate_up_weight)))
        )
    for b in batches:
        mlp_own = queue_scatter_sum(dot_nn(activated[b], down_weight))
        outputs.append((middle_own[b] + mlp_own.astype(F32)).astype(BF16))

    activated_all = jnp.concatenate(activated, 0)
    grads_in_all = jnp.concatenate(grads_in, 0)
    down_sum = owner_sums(lambda f: dot_tn(activated_all, owner_block(grads_in_all, f, 1)))
    normed_two_all = jnp.concatenate(normed_two, 0)
    grad_pair_all = jnp.concatenate(grad_pair, 0)
    pair_sum = owner_sums(lambda f: dot_tn(owner_block(normed_two_all, f, 1), grad_pair_all))

    gain_one_own = lax.dynamic_slice_in_dim(gain_one, column_start, local_width, 0)
    norm_sum_one = jnp.zeros((full_width,), F32)
    norm_sum_two = jnp.zeros((full_width,), F32)
    input_grads, middle_low, grad_projected = [], [], []
    for b in batches:
        grad_two = grad_normed_two[b].astype(F32)
        norm_sum_two = norm_sum_two + jnp.sum(grad_two * middle[b] * scale_two[b], 0)
        scaled_two = grad_two * gain_two
        grad_middle = (
            grads_in[b].astype(F32)
            + scale_two[b] * scaled_two
            - middle[b]
            * (scale_two[b] * scale_two[b] * scale_two[b])
            * jnp.mean(scaled_two * middle[b], -1, keepdims=True)
        )
        middle_low.append(grad_middle.astype(BF16))
        grad_heads = (
            dot_nt(middle_low[b], out_weight)
            .astype(BF16)
            .reshape(row_count, head_count, HEAD_SIZE)
        )
        grad_query_rot, grad_keys, grad_values = attend_backward(
            cut(query_rotated, b),
            keys[b],
            values[b],
            allowed[b],
            totals[b],
            heads[b],
            grad_heads,
            score_scale,
        )
        grad_window = jnp.concatenate([grad_keys, grad_values], -1)
        own_pairs = grad_window[back * row_count :]
        for o in range(1, back + 1):
            block = grad_window[(back - o) * row_count : (back - o + 1) * row_count]
            own_pairs = own_pairs + passed_along(
                block.astype(BF16), "fsdp", -o * stride
            ).astype(F32)
        cosine_b, sine_b = cut(cosine_table, b), cut(sine_lookup, b)
        grad_query_low = (
            reverse_rotary(grad_query_rot, cosine_b, sine_b)
            .reshape(row_count, query_width)
            .astype(BF16)
        )
        grad_key_low = reverse_rotary(own_pairs[:, None, :HEAD_SIZE], cosine_b, sine_b)[
            :, 0
        ].astype(BF16)
        grad_value_low = own_pairs[:, HEAD_SIZE:].astype(BF16)
        grad_projected.append(
            jnp.concatenate([grad_query_low, grad_key_low, grad_value_low], 1)
        )
        grad_one = dot_nt(grad_projected[b], project_weight)
        weighted = grad_one * inputs[b]
        norm_sum_one = norm_sum_one + jnp.sum(weighted * scale_one[b], 0)
        row_term = jnp.sum(weighted * gain_one, -1, keepdims=True) / full_width
        row_high = row_term.astype(BF16)
        row_low = (row_term - row_high.astype(F32)).astype(BF16)
        extra = jnp.pad(
            jnp.concatenate([row_high, row_low], 1), ((0, 0), (0, GAIN_COLUMNS - 2))
        )
        slots = grad_one.astype(BF16).reshape(row_count, -1, local_width)
        extra = jnp.broadcast_to(extra[:, None], (row_count, slots.shape[1], GAIN_COLUMNS))
        summed = queue_scatter_sum(jnp.concatenate([slots, extra], 2).reshape(row_count, -1))
        row_mean = jnp.sum(summed[:, local_width : local_width + 2].astype(F32), 1, keepdims=True)
        grad_middle_own = lax.dynamic_slice_in_dim(grad_middle, column_start, local_width, 1)
        input_grads.append(
            grad_middle_own
            + scale_one[b] * (summed[:, :local_width].astype(F32) * gain_one_own)
            - tokens[b].astype(F32) * (scale_one[b] * scale_one[b] * scale_one[b]) * row_mean
        )
    heads_all = jnp.concatenate([h.reshape(row_count, query_width) for h in heads], 0)
    middle_low_all = jnp.concatenate(middle_low, 0)
    out_sum = owner_sums(lambda f: dot_tn(heads_all, owner_block(middle_low_all, f, 1)))
    grad_projected_all = jnp.concatenate(grad_projected, 0)
    project_sum = owner_sums(
        lambda f: dot_tn(owner_block(normed_one, f, 1), grad_projected_all)
    )
    norm_sum_one = lax.psum(norm_sum_one, ("fsdp", "tp"))
    norm_sum_two = lax.psum(norm_sum_two, "fsdp")
    index = lax.axis_index("fsdp")
    grad_scale = (batch_count * row_count * lax.axis_size("fsdp")) ** (-0.5)
    return (
        jnp.stack(outputs),
        jnp.stack(input_grads),
        owner_block(norm_sum_one, index, 0) * grad_scale,
        project_sum[:, :query_width] * grad_scale,
        project_sum[:, query_width : query_width + HEAD_SIZE] * grad_scale,
        project_sum[:, query_width + HEAD_SIZE :] * grad_scale,
        out_sum * grad_scale,
        owner_block(norm_sum_two, index, 0) * grad_scale,
        pair_sum[:, :hidden] * grad_scale,
        pair_sum[:, hidden:] * grad_scale,
        down_sum * grad_scale,
    )


def solution(mesh):
    in_specs = (
        P(None, "fsdp", "tp"),
        P(None, "fsdp", "tp"),
        P(None, "fsdp"),
        P(None, "fsdp"),
        P("fsdp"),
        P("fsdp", "tp"),
        P("fsdp", "tp"),
        P("fsdp", "tp"),
        P("tp", "fsdp"),
        P("fsdp"),
        P("fsdp", "tp"),
        P("fsdp", "tp"),
        P("tp", "fsdp"),
    )
    out_specs = (
        P(None, "fsdp", "tp"),
        P(None, "fsdp", "tp"),
        P("fsdp"),
        P("fsdp", "tp"),
        P("fsdp", "tp"),
        P("fsdp", "tp"),
        P("tp", "fsdp"),
        P("fsdp"),
        P("fsdp", "tp"),
        P("fsdp", "tp"),
        P("tp", "fsdp"),
    )
    return jax.shard_map(shards, mesh=mesh, in_specs=in_specs, out_specs=out_specs, check_vma=False)
```

time: 1470 us -> 793 us (0.54)
  waiting for transfers between devices: 940 us -> 248 us
  starting transfers between devices: 117 us -> 59.2 us
  local copies, waits for them, and re-layouts: 26.4 us -> 76.6 us
  matrix products: 221 us -> 247 us
    reduce_scatter x11 -> x4, waiting for transfers between devices: 387 us -> 27.4 us  [queue_scatter_sum(): lax.psum_scatter(partial.astype(BF16), 'tp', scatter_dimension=1, tiled=T...]
    psum x2 -> x0, waiting for transfers between devices: 297 us -> none  [back_sum(): return lax.psum(partial_term, 'tp')]
    all_gather x11 -> x8, waiting for transfers between devices: 245 us -> 16.5 us  [the longest x4 11.2 us: queue_gather(): return lax.all_gather(part, 'tp', axis=1, tiled=True)]
    ppermute x0 -> x28, waiting for transfers between devices: none -> 202 us  [exchange(): lax.ppermute(block, axis, [(i, i ^ mask) for i in range(lax.axis_size(axi...]
    ppermute x70 -> x12, starting transfers between devices: 115 us -> 23.6 us  [passed_along(): return lax.ppermute(block, axis, route)]
    psum x0 -> x2, blocking collectives: none -> 55.9 us  [the longest x1 40.9 us: shards(): norm_sum_one = lax.psum(norm_sum_one, ('fsdp', 'tp'))]
    all_gather x4 -> x0, blocking collectives: 35.5 us -> none  [the longest x1 9.51 us: shards(): lax.all_gather(attn_norm, 'fsdp', axis=0, tiled=True)]
    ppermute x0 -> x28, starting transfers between devices: none -> 34.8 us  [exchange(): lax.ppermute(block, axis, [(i, i ^ mask) for i in range(lax.axis_size(axi...]
  transfers between devices with their start and end apart: 94 -> 54, of which waited for: 24 -> 17; matrix products, arithmetic and copies ran while one was open for 19% -> 45% of each run, Pallas kernels for 0% -> 0%
where the time goes in v1:
time: 793 us; the launch traced here: 783 us
  waiting for transfers between devices  248 us (31%)
  matrix products  247 us (31%)
  other arithmetic  79.7 us (10%)
  local copies, waits for them, and re-layouts  76.6 us (10%)
  starting transfers between devices  59.2 us (7%)
  blocking collectives  55.9 us (7%)
  between operations  16.9 us (2%)
    ppermute x28, waiting for transfers between devices, exchange(): lax.ppermute(block, axis, [(i, i ^ mask) for i in range(lax.axis_size(axi...  202 us
    dot_general x32, matrix products, dot_tn(): lax.dot_general(left, right, (((0,), (0,)), ((), ())), preferred_element_...  130 us
    dot_general x9, matrix products, dot_nn(): return jnp.dot(left, right, preferred_element_type=F32)  44.2 us
    psum x1, blocking collectives, shards(): norm_sum_one = lax.psum(norm_sum_one, ('fsdp', 'tp'))  40.9 us
    ppermute x28, starting transfers between devices, exchange(): lax.ppermute(block, axis, [(i, i ^ mask) for i in range(lax.axis_size(axi...  34.8 us
    reduce_scatter x4, waiting for transfers between devices, queue_scatter_sum(): lax.psum_scatter(partial.astype(BF16), 'tp', scatter_dimension=1, tiled=T...  27.4 us
    unnamed x292, local copies, waits for them, and re-layouts  26.2 us
    ppermute x12, starting transfers between devices, passed_along(): return lax.ppermute(block, axis, route)  23.6 us
  transfers between devices with their start and end apart: 54, of which 17 were waited for; matrix products, arithmetic and copies ran while one was open for 45% of the time, Pallas kernels for 0%

profile of v1, /device:TPU:0, one launch (start us, length us, event | category | flops | bytes accessed | tf_op | source)
XLA Modules:
  0.0 783.3 jit_solution(5329243567917569479)
XLA Ops:
  20.5 22.3 %collective-permute-done = bf16[1,256,512]{2,1,0:T(8,128)(2,1)S(1)} collective-permute-done((bf16[1,256,512]{2,1,0:T(8,128)(2,1)S(1)}, bf16[1,256,512]{2,1,0:T(8,128)(2,1)S(1)}, u32[]{:S(2)}, u32[]{:S(2)}) %collective-permute-start) | collective-permute-done | bytes 262176 | tf_op jit(solution)/shard_map/ppermute | solution.py:56
  47.0 10.7 %collective-permute-done.1 = bf16[2,1,256,512]{3,2,0,1:T(8,128)(2,1)S(1)} collective-permute-done((bf16[2,1,256,512]{3,2,0,1:T(8,128)(2,1)S(1)}, bf16[2,1,256,512]{3,2,0,1:T(8,128)(2,1)S(1)}, u32[]{:S(2)}, u32[]{:S(2)}) %collective-permute-start.1) | collective-permute-done | bytes 524320 | tf_op jit(solution)/shard_map/ppermute | solution.py:56
  144.5 14.6 %collective-permute-done.8 = bf16[256,2,512]{2,0,1:T(8,128)(2,1)S(1)} collective-permute-done((bf16[256,2,512]{2,0,1:T(8,128)(2,1)S(1)}, bf16[256,2,512]{2,0,1:T(8,128)(2,1)S(1)}, u32[]{:S(2)}, u32[]{:S(2)}) %collective-permute-start.8) | collective-permute-done | bytes 524320 | tf_op jit(solution)/shard_map/ppermute | solution.py:56
  161.1 27.0 %collective-permute-done.9 = bf16[256,1,512]{2,0,1:T(8,128)(2,1)S(1)} collective-permute-done((bf16[256,1,512]{2,0,1:T(8,128)(2,1)S(1)}, bf16[256,1,512]{2,0,1:T(8,128)(2,1)S(1)}, u32[]{:S(2)}, u32[]{:S(2)}) %collective-permute-start.9) | collective-permute-done | bytes 262176 | tf_op jit(solution)/shard_map/ppermute | solution.py:56
  188.5 14.2 %collective-permute-done.10 = bf16[1,256,512]{2,1,0:T(8,128)(2,1)S(1)} collective-permute-done((bf16[1,256,512]{2,1,0:T(8,128)(2,1)S(1)}, bf16[1,256,512]{2,1,0:T(8,128)(2,1)S(1)}, u32[]{:S(2)}, u32[]{:S(2)}) %collective-permute-start.10) | collective-permute-done | bytes 262176 | tf_op jit(solution)/shard_map/ppermute | solution.py:56
  203.0 13.8 %collective-permute-done.11 = bf16[2,1,256,512]{3,2,1,0:T(8,128)(2,1)S(1)} collective-permute-done((bf16[2,1,256,512]{3,2,1,0:T(8,128)(2,1)S(1)}, bf16[2,1,256,512]{3,2,1,0:T(8,128)(2,1)S(1)}, u32[]{:S(2)}, u32[]{:S(2)}) %collective-permute-start.11) | collective-permute-done | bytes 524320 | tf_op jit(solution)/shard_map/ppermute | solution.py:56
  225.9 9.4 %fusion.379 = f32[256,2816]{1,0:T(8,128)} fusion(bf16[256,2048]{1,0:T(8,128)(2,1)} %multiply_convert_fusion.1, bf16[2048,2816]{1,0:T(8,128)(2,1)} %all-gather.15.cloned.1.call-done), kind=kOutput, calls=%fused_computation.601 | convolution fusion | flops 2952790016 | bytes 15466496 | tf_op jit(solution)/shard_map/dot_general | solution.py:44
  251.9 27.4 %reduce-scatter.15.cloned.1.call-done = bf16[256,512]{1,0:T(8,128)(2,1)} async-done(((bf16[256,2048]{1,0:T(8,128)(2,1)}), bf16[256,512]{1,0:T(8,128)(2,1)}) %reduce-scatter.15.cloned.1.call-update) | async-done | bytes 262160 | tf_op jit(solution)/shard_map/reduce_scatter | solution.py:108
  280.3 17.4 %collective-permute-done.14 = bf16[1,256,512]{2,1,0:T(8,128)(2,1)S(1)} collective-permute-done((bf16[1,256,512]{2,1,0:T(8,128)(2,1)S(1)}, bf16[1,256,512]{2,1,0:T(8,128)(2,1)S(1)}, u32[]{:S(2)}, u32[]{:S(2)}) %collective-permute-start.14) | collective-permute-done | bytes 262176 | tf_op jit(solution)/shard_map/ppermute | solution.py:56
  300.6 19.9 %collective-permute-done.15 = bf16[2,1,256,512]{3,2,0,1:T(8,128)(2,1)S(1)} collective-permute-done((bf16[2,1,256,512]{3,2,0,1:T(8,128)(2,1)S(1)}, bf16[2,1,256,512]{3,2,0,1:T(8,128)(2,1)S(1)}, u32[]{:S(2)}, u32[]{:S(2)}) %collective-permute-start.15) | collective-permute-done | bytes 524320 | tf_op jit(solution)/shard_map/ppermute | solution.py:56
  335.6 9.1 %fusion.380 = f32[256,2816]{1,0:T(8,128)} fusion(bf16[256,2048]{1,0:T(8,128)(2,1)S(1)} %get-tuple-element.121, bf16[2048,2816]{1,0:T(8,128)(2,1)} %all-gather.15.cloned.1.call-done), kind=kOutput, calls=%fused_computation.602 | convolution fusion | flops 2952790016 | bytes 15466496 | tf_op jit(solution)/shard_map/dot_general | solution.py:44
  411.0 12.2 %fusion.27 = bf16[1,256,2816]{2,1,0:T(8,128)(2,1)} fusion(s32[]{:T(128)S(6)} %select_n.341, bf16[256,2048]{1,0:T(8,128)(2,1)S(1)} %copy-done.51, bf16[256,2048]{1,0:T(8,128)(2,1)S(1)} %copy-done.71, bf16[256,1408]{1,0:T(8,128)(2,1)S(1)} %copy-done.132, bf16[256,1408]{1,0:T(8,128)(2,1)S(1)} %copy-done.128, bf16[256,1408]{1,0:T(8,128)(2,1)S(1)} %copy-done.124, ...), kind=kOutput, calls=%fused_computation.105 | convolution fusion | flops 750977024 | bytes 6422532 | tf_op jit(solution)/shard_map/dot_general | solution.py:52
  423.2 12.2 %fusion.26 = bf16[1,256,2816]{2,1,0:T(8,128)(2,1)} fusion(s32[]{:T(128)S(6)} %select_n.340, bf16[256,2048]{1,0:T(8,128)(2,1)S(1)} %copy-done.51, bf16[256,2048]{1,0:T(8,128)(2,1)S(1)} %copy-done.71, bf16[256,1408]{1,0:T(8,128)(2,1)S(1)} %copy-done.132, bf16[256,1408]{1,0:T(8,128)(2,1)S(1)} %copy-done.128, bf16[256,1408]{1,0:T(8,128)(2,1)S(1)} %copy-done.124, ...), kind=kOutput, calls=%fused_computation.104 | convolution fusion | flops 750977024 | bytes 6422532 | tf_op jit(solution)/shard_map/dot_general | solution.py:52
  435.4 12.3 %fusion.25 = bf16[1,256,2816]{2,1,0:T(8,128)(2,1)} fusion(s32[]{:T(128)S(6)} %select_n.339, bf16[256,2048]{1,0:T(8,128)(2,1)S(1)} %copy-done.51, bf16[256,2048]{1,0:T(8,128)(2,1)S(1)} %copy-done.71, bf16[256,1408]{1,0:T(8,128)(2,1)S(1)} %copy-done.132, bf16[256,1408]{1,0:T(8,128)(2,1)S(1)} %copy-done.128, bf16[256,1408]{1,0:T(8,128)(2,1)S(1)} %copy-done.124, ...), kind=kOutput, calls=%fused_computation.103 | convolution fusion | flops 750977024 | bytes 6422532 | tf_op jit(solution)/shard_map/dot_general | solution.py:52
  447.7 12.2 %fusion.24 = bf16[1,256,2816]{2,1,0:T(8,128)(2,1)} fusion(s32[]{:T(128)S(6)} %select_n.338, bf16[256,2048]{1,0:T(8,128)(2,1)S(1)} %copy-done.51, bf16[256,2048]{1,0:T(8,128)(2,1)S(1)} %copy-done.71, bf16[256,1408]{1,0:T(8,128)(2,1)S(1)} %copy-done.132, bf16[256,1408]{1,0:T(8,128)(2,1)S(1)} %copy-done.128, bf16[256,1408]{1,0:T(8,128)(2,1)S(1)} %copy-done.124, ...), kind=kOutput, calls=%fused_computation.102 | convolution fusion | flops 750977024 | bytes 6422532 | tf_op jit(solution)/shard_map/dot_general | solution.py:52
  481.5 10.6 %all-gather.21.cloned.1.call-done = bf16[256,2048]{1,0:T(8,128)(2,1)} async-done(((bf16[256,512]{1,0:T(8,128)(2,1)}), bf16[256,2048]{1,0:T(8,128)(2,1)}) %all-gather.21.cloned.1.call-update) | async-done | bytes 1048592 | tf_op jit(solution)/shard_map/all_gather | solution.py:104
  570.1 15.0 %psum.15 = f32[2048]{0:T(1024)S(1)} all-reduce(f32[2048]{0:T(1024)S(1)} %add.414), channel_id=1, replica_groups=mesh['fsdp'=8,'tp'=4] {'fsdp'}, use_global_device_ids=true, to_apply=%region_27.28 | all-reduce | flops 2048 | bytes 16384 | tf_op jit(solution)/shard_map/psum | solution.py:356
  600.0 40.9 %psum.14 = f32[2048]{0:T(1024)S(1)} all-reduce(f32[2048]{0:T(1024)S(1)} %add.391), channel_id=1, replica_groups=mesh['fsdp'=8,'tp'=4] {'fsdp','tp'}, use_global_device_ids=true, to_apply=%region_24.25 | all-reduce | flops 2048 | bytes 16384 | tf_op jit(solution)/shard_map/psum | solution.py:355
  657.5 13.4 %fusion.29 = bf16[256,2816]{1,0:T(8,128)(2,1)} fusion(bf16[4,256,2816]{2,1,0:T(8,128)(2,1)} %collective-permute-done.32, s32[]{:T(128)S(6)} %select_n.343, bf16[256,2048]{1,0:T(8,128)(2,1)S(1)} %copy-done.52, bf16[256,2048]{1,0:T(8,128)(2,1)S(1)} %copy-done.72, bf16[256,1408]{1,0:T(8,128)(2,1)S(1)} %copy-done.133, bf16[256,1408]{1,0:T(8,128)(2,1)S(1)} %copy-done.129, ...), kind=kOutput, calls=%fused_computation.111 | convolution fusion | flops 752418816 | bytes 7864324 | tf_op jit(solution)/shard_map/dot_general | solution.py:52
  670.8 13.5 %fusion.30 = bf16[256,2816]{1,0:T(8,128)(2,1)} fusion(bf16[4,256,2816]{2,1,0:T(8,128)(2,1)} %collective-permute-done.32, s32[]{:T(128)S(6)} %select_n.342, bf16[256,2048]{1,0:T(8,128)(2,1)S(1)} %copy-done.52, bf16[256,2048]{1,0:T(8,128)(2,1)S(1)} %copy-done.72, bf16[256,1408]{1,0:T(8,128)(2,1)S(1)} %copy-done.133, bf16[256,1408]{1,0:T(8,128)(2,1)S(1)} %copy-done.129, ...), kind=kOutput, calls=%fused_computation.113 | convolution fusion | flops 752418816 | bytes 7864324 | tf_op jit(solution)/shard_map/dot_general | solution.py:52
  685.2 13.6 %fusion.31 = bf16[256,2816]{1,0:T(8,128)(2,1)} fusion(bf16[4,256,2816]{2,1,0:T(8,128)(2,1)} %collective-permute-done.32, s32[]{:T(128)S(6)} %select_n.337, bf16[256,2048]{1,0:T(8,128)(2,1)S(1)} %copy-done.52, bf16[256,2048]{1,0:T(8,128)(2,1)S(1)} %copy-done.72, bf16[256,1408]{1,0:T(8,128)(2,1)S(1)} %copy-done.133, bf16[256,1408]{1,0:T(8,128)(2,1)S(1)} %copy-done.129, ...), kind=kOutput, calls=%fused_computation.115 | convolution fusion | flops 752418816 | bytes 7864324 | tf_op jit(solution)/shard_map/dot_general | solution.py:52
  715.1 19.4 %collective-permute-done.33 = bf16[256,2816]{1,0:T(8,128)(2,1)} collective-permute-done((bf16[256,2816]{1,0:T(8,128)(2,1)}, bf16[256,2816]{1,0:T(8,128)(2,1)}, u32[]{:S(2)}, u32[]{:S(2)}) %collective-permute-start.33) | collective-permute-done | bytes 1441824 | tf_op jit(solution)/shard_map/ppermute | solution.py:56
  734.5 26.5 %collective-permute-done.34 = bf16[256,2816]{1,0:T(8,128)(2,1)} collective-permute-done((bf16[256,2816]{1,0:T(8,128)(2,1)}, bf16[256,2816]{1,0:T(8,128)(2,1)}, u32[]{:S(2)}, u32[]{:S(2)}) %collective-permute-start.34) | collective-permute-done | bytes 1441824 | tf_op jit(solution)/shard_map/ppermute | solution.py:56
  761.0 13.6 %fusion.28 = f32[256,2816]{1,0:T(8,128)S(1)} fusion(bf16[256,2816]{1,0:T(8,128)(2,1)} %collective-permute-done.35, bf16[256,2816]{1,0:T(8,128)(2,1)} %collective-permute-done.34, bf16[256,2816]{1,0:T(8,128)(2,1)} %collective-permute-done.33, bf16[4,256,2816]{2,1,0:T(8,128)(2,1)} %collective-permute-done.32, s32[]{:T(128)S(6)} %select_n.336, ...), kind=kOutput, calls=%fused_computation.109 | convolution fusion | flops 756023296 | bytes 13631492 | tf_op jit(solution)/shard_map/dot_general | solution.py:52
  (597 shorter events, 365.4 us)
Async XLA Ops:
  7.2 73.4 %all-gather.13.cloned.1.call-start = ((), (), s32[]{:S(2)}) async-start(), calls=%async_computation.7 | async-start | bytes 2359296 | tf_op jit(solution)/shard_map/all_gather | solution.py:206
  7.9 76.5 %all-gather.11.cloned.1.call-start = ((), (), s32[]{:S(2)}) async-start(), calls=%async_computation.6 | async-start | bytes 3538944 | tf_op jit(solution)/shard_map/all_gather | solution.py:201
  13.1 212.9 %all-gather.15.cloned.1.call-start = ((), (), s32[]{:S(2)}) async-start(), calls=%async_computation.8 | async-start | bytes 12976128 | tf_op jit(solution)/shard_map/all_gather | solution.py:207
  14.4 220.9 %all-gather.23.cloned.1.call-start = ((), (), s32[]{:S(2)}) async-start(), calls=%async_computation.16 | async-start | bytes 1310720 | tf_op jit(solution)/shard_map/all_gather | solution.py:104
  15.3 225.3 %all-gather.17.cloned.1.call-start = ((), (), s32[]{:S(2)}) async-start(), calls=%async_computation.9 | async-start | bytes 6488064 | tf_op jit(solution)/shard_map/all_gather | solution.py:210
  19.7 259.6 %reduce-scatter.15.cloned.1.call-start = ((), (), s32[]{:S(2)}) async-start(), calls=%async_computation.12 | async-start | bytes 1310720 | tf_op jit(solution)/shard_map/reduce_scatter | solution.py:108
  251.8 75.8 %all-gather.19.cloned.1.call-start = ((), (), s32[]{:S(2)}) async-start(), calls=%async_computation.13 | async-start | bytes 1310720 | tf_op jit(solution)/shard_map/all_gather | solution.py:104
  279.3 66.0 %all-gather.25.cloned.1.call-start = ((), (), s32[]{:S(2)}) async-start(), calls=%async_computation.17 | async-start | bytes 1310720 | tf_op jit(solution)/shard_map/all_gather | solution.py:104
  300.5 159.4 %reduce-scatter.17.cloned.1.call-start = ((), (), s32[]{:S(2)}) async-start(), calls=%async_computation.14 | async-start | bytes 1310720 | tf_op jit(solution)/shard_map/reduce_scatter | solution.py:108
  361.7 111.2 %reduce-scatter.11.cloned.1.call-start = ((), (), s32[]{:S(2)}) async-start(), calls=%async_computation.10 | async-start | bytes 1310720 | tf_op jit(solution)/shard_map/reduce_scatter | solution.py:108
  369.1 103.8 %reduce-scatter.13.cloned.1.call-start = ((), (), s32[]{:S(2)}) async-start(), calls=%async_computation.11 | async-start | bytes 1310720 | tf_op jit(solution)/shard_map/reduce_scatter | solution.py:108
  375.4 100.8 %collective-permute-start.36 = (bf16[4,1408,256]{2,1,0:T(8,128)(2,1)}, bf16[4,1408,256]{2,1,0:T(8,128)(2,1)}, u32[]{:S(2)}, u32[]{:S(2)}) collective-permute-start(bf16[4,1408,256]{2,1,0:T(8,128)(2,1)} %pad_maximum_fusion.2), channel_id=1, source_target_pairs={{0,4},{4,0},{8,12},{12,8},{16,20},{20,16},{24,28},{28,24},{1,5},{5... | collective-permute-start | bytes 8650760 | tf_op jit(solution)/shard_map/ppermute | solution.py:56
  399.5 92.6 %all-gather.21.cloned.1.call-start = ((), (), s32[]{:S(2)}) async-start(), calls=%async_computation.15 | async-start | bytes 1310720 | tf_op jit(solution)/shard_map/all_gather | solution.py:104
  405.4 63.1 %collective-permute-start.16 = (bf16[256,128]{1,0:T(8,128)(2,1)}, bf16[256,128]{1,0:T(8,128)(2,1)}, u32[]{:S(2)}, u32[]{:S(2)}) collective-permute-start(bf16[256,128]{1,0:T(8,128)(2,1)} %get-tuple-element.97), channel_id=1, source_target_pairs={{4,0},{8,4},{12,8},{16,12},{20,16},{24,20},{28,24},{5,1},{9,5},{13... | collective-permute-start | bytes 196616 | tf_op jit(solution)/shard_map/ppermute | solution.py:62
  406.7 62.9 %collective-permute-start.19 = (bf16[256,128]{1,0:T(8,128)(2,1)}, bf16[256,128]{1,0:T(8,128)(2,1)}, u32[]{:S(2)}, u32[]{:S(2)}) collective-permute-start(bf16[256,128]{1,0:T(8,128)(2,1)} %get-tuple-element.98), channel_id=1, source_target_pairs={{16,0},{20,4},{24,8},{28,12},{17,1},{21,5},{25,9},{29,13},{18,2},{... | collective-permute-start | bytes 196616 | tf_op jit(solution)/shard_map/ppermute | solution.py:62
  408.0 61.6 %collective-permute-start.18 = (bf16[256,128]{1,0:T(8,128)(2,1)S(1)}, bf16[256,128]{1,0:T(8,128)(2,1)}, u32[]{:S(2)}, u32[]{:S(2)}) collective-permute-start(bf16[256,128]{1,0:T(8,128)(2,1)S(1)} %get-tuple-element.99), channel_id=1, source_target_pairs={{12,0},{16,4},{20,8},{24,12},{28,16},{13,1},{17,5},{21,9},{25,13},... | collective-permute-start | bytes 196616 | tf_op jit(solution)/shard_map/ppermute | solution.py:62
  409.3 60.3 %collective-permute-start.17 = (bf16[256,128]{1,0:T(8,128)(2,1)S(1)}, bf16[256,128]{1,0:T(8,128)(2,1)}, u32[]{:S(2)}, u32[]{:S(2)}) collective-permute-start(bf16[256,128]{1,0:T(8,128)(2,1)S(1)} %get-tuple-element.100), channel_id=1, source_target_pairs={{8,0},{12,4},{16,8},{20,12},{24,16},{28,20},{9,1},{13,5},{17,9},{2... | collective-permute-start | bytes 196616 | tf_op jit(solution)/shard_map/ppermute | solution.py:62
  459.9 248.2 %reduce-scatter.21.cloned.1.call-start = ((), (), s32[]{:S(2)}) async-start(), calls=%async_computation.19 | async-start | bytes 1638400
  468.4 187.6 %collective-permute-start.32 = (bf16[4,256,2816]{2,1,0:T(8,128)(2,1)}, bf16[4,256,2816]{2,1,0:T(8,128)(2,1)}, u32[]{:S(2)}, u32[]{:S(2)}) collective-permute-start(bf16[4,256,2816]{2,1,0:T(8,128)(2,1)} %pad_maximum_fusion), channel_id=1, source_target_pairs={{0,4},{4,0},{8,12},{12,8},{16,20},{20,16},{24,28},{28,24},{1,5},{5... | collective-permute-start | bytes 17301512 | tf_op jit(solution)/shard_map/ppermute | solution.py:56
  562.8 147.0 %reduce-scatter.19.cloned.1.call-start = ((), (), s32[]{:S(2)}) async-start(), calls=%async_computation.18 | async-start | bytes 1638400
  569.8 71.7 %collective-permute-start.28 = (bf16[4,512,256]{2,1,0:T(8,128)(2,1)}, bf16[4,512,256]{2,1,0:T(8,128)(2,1)}, u32[]{:S(2)}, u32[]{:S(2)}) collective-permute-start(bf16[4,512,256]{2,1,0:T(8,128)(2,1)} %pad_maximum_fusion.10), channel_id=1, source_target_pairs={{0,4},{4,0},{8,12},{12,8},{16,20},{20,16},{24,28},{28,24},{1,5},{5... | collective-permute-start | bytes 3145736 | tf_op jit(solution)/shard_map/ppermute | solution.py:56
  590.6 58.9 %collective-permute-start.24 = (bf16[4,256,640]{2,1,0:T(8,128)(2,1)}, bf16[4,256,640]{2,1,0:T(8,128)(2,1)}, u32[]{:S(2)}, u32[]{:S(2)}) collective-permute-start(bf16[4,256,640]{2,1,0:T(8,128)(2,1)} %pad_maximum_fusion.8), channel_id=1, source_target_pairs={{0,4},{4,0},{8,12},{12,8},{16,20},{20,16},{24,28},{28,24},{1,5},{5... | collective-permute-start | bytes 3932168 | tf_op jit(solution)/shard_map/ppermute | solution.py:56
  700.3 60.7 %collective-permute-start.34 = (bf16[256,2816]{1,0:T(8,128)(2,1)}, bf16[256,2816]{1,0:T(8,128)(2,1)}, u32[]{:S(2)}, u32[]{:S(2)}) collective-permute-start(bf16[256,2816]{1,0:T(8,128)(2,1)} %fusion.30), channel_id=1, source_target_pairs={{0,16},{4,20},{8,24},{12,28},{16,0},{20,4},{24,8},{28,12},{1,17},{... | collective-permute-start | bytes 4325384 | tf_op jit(solution)/shard_map/ppermute | solution.py:56
  701.5 59.5 %collective-permute-start.35 = (bf16[256,2816]{1,0:T(8,128)(2,1)}, bf16[256,2816]{1,0:T(8,128)(2,1)}, u32[]{:S(2)}, u32[]{:S(2)}) collective-permute-start(bf16[256,2816]{1,0:T(8,128)(2,1)} %fusion.29), channel_id=1, source_target_pairs={{0,8},{4,12},{8,0},{12,4},{16,24},{20,28},{24,16},{28,20},{1,9},{5... | collective-permute-start | bytes 4325384 | tf_op jit(solution)/shard_map/ppermute | solution.py:56
  (167 other events, 2151.1 us)
Sparse Core Ops, SparseCore 0:
  9.9 30.8 all-gather.12
  43.2 32.1 all-gather.10
  77.9 68.7 all-gather.14
  148.7 42.5 all-gather.22
  193.0 47.5 all-gather.16
  251.9 27.2 reduce-scatter.14
  280.8 33.2 all-gather.18
  316.2 29.0 all-gather.24
  361.9 26.6 reduce-scatter.16
  391.3 25.7 reduce-scatter.10
  419.4 25.7 reduce-scatter.12
  460.1 31.9 all-gather.20
  562.9 31.5 reduce-scatter.20
  600.1 31.0 reduce-scatter.18
